TPU v7x, 32 devices: a whole 2x2x4 slice. The times are simulated.
32 devices in a mesh: query: 2 (over y), dom: 16 (over z, x, core).
Axes of the slice: x: 2, y: 2, z: 4, core: 2. Of those that a mesh axis runs over, the one named last changes fastest.
Arguments:
- h_in: bfloat16 [4096, 256], P('dom', 'query'), may hold values from -6 to 6
- cotangent: bfloat16 [4096, 256], P('dom', 'query'), may hold values from -6 to 6
- w_one: bfloat16 [64, 64], replicated, may hold values from -0.75 to 0.75
- w_two: bfloat16 [64, 64], replicated, may hold values from -0.75 to 0.75
- rel_one: bfloat16 [535, 64], replicated, may hold values from -3 to 3
- rel_two: bfloat16 [535, 64], replicated, may hold values from -3 to 3
- query_emb: bfloat16 [535, 64], replicated, may hold values from -6 to 6
- q_head: int32 [4], P('query'), may hold values from 0 to 4095
- q_rel: int32 [4], P('query'), may hold values from 0 to 534
- bnd_rows: int32 [1024], P('dom'), may hold values from 0 to 255
- ghost_slots: int32 [256, 16], P('dom'), may hold values from 0 to 63
- edges_in: int32 [3, 16384], P(None, 'dom'), may hold values from 0 to 535, as said below
- edges_bd: int32 [3, 16384], P(None, 'dom'), may hold values from 0 to 535, as said below
Outputs:
- grad_in: float32 [4096, 256], P('dom', 'query')
- grad_w: float32 [2, 64, 64], replicated
- grad_rel: float32 [2, 535, 64], replicated
Inputs may be any that keep to these rules, and one draw needn't show every extreme that they name: `edges_in`: row 0 is a local source row, row 1 a local destination row, row 2 a relation; relation 535 marks padding, which follows all real edges in each partition's block of 1024; at least a quarter of each block is real and some partition's block has no padding. `edges_bd`: row 0 is a ghost index below 256, row 1 a local destination row, row 2 a relation; relation 535 marks padding, which follows all real edges in each partition's block of 1024; at least a quarter of each block is real and some partition's block has no padding.
All inputs are finite; a program needn't handle non-finite values.
Results may differ from a plain program's by a relative error of at most 0.0049.
The roundings to bfloat16 on the way count: a program that leaves them out, or rounds other values in their place, can miss the bound.
Values may be sent and summed in bfloat16 or wider, within the bound.
A program may use at most 64 MiB of HBM per device.

v0:
```python
import functools
import math

import jax
import jax.numpy as jnp
from jax import lax
from jax.experimental import pallas as pl
from jax.experimental.pallas import tpu as pltpu
from jax.sharding import PartitionSpec as P

MESH = pl.DeviceIdType.MESH
F32 = jnp.float32
BF16 = jnp.bfloat16
CHUNK = 16


def dot_nn(a, b):
    return lax.dot_general(a, b, (((1,), (0,)), ((), ())), preferred_element_type=F32)


def dot_nt(a, b):
    return lax.dot_general(a, b, (((1,), (1,)), ((), ())), preferred_element_type=F32)


def split_hi_lo(x, axis):
    hi = x.astype(BF16)
    lo = (x - hi.astype(F32)).astype(BF16)
    return jnp.concatenate([hi, lo], axis=axis)


def onehot_into(dest, ids, col0, block):
    rows = dest.shape[0]
    count = ids.shape[1]

    def fill(i, carry):
        base = pl.multiple_of(i * block, block)
        row_ids = lax.broadcasted_iota(jnp.int32, (block, count), 0) + base
        dest[pl.ds(base, block), pl.ds(col0, count)] = jnp.where(row_ids == ids, 1.0, 0.0).astype(BF16)
        return carry

    lax.fori_loop(0, rows // block, fill, 0)


def kernel(
    n_q,
    n_d,
    scale_w,
    scale_r,
    rel_count,
    rel_rows,
    h_ref,
    cot_ref,
    w1_ref,
    w2_ref,
    relt_ref,
    qhead_ref,
    qrel_ref,
    bnd_ref,
    gs_ref,
    ein_ref,
    ebd_ref,
    gin_ref,
    gw_ref,
    grel_ref,
    rt,
    vt,
    st_in,
    st_bd,
    rel_e,
    x1,
    x2,
    req,
    out1,
    ghost1,
    out2,
    ghost2,
    ret_out2,
    ret_in2,
    ret_out1,
    ret_in1,
    red_src,
    red_in,
    red_sum,
    red_all,
    xsend,
    xrecv,
    rsend,
    rrecv,
    gsend,
    grecv,
):
    me_d = lax.axis_index("dom")
    me_q = lax.axis_index("query")
    total = n_q * n_d
    lin = me_q * n_d + me_d
    feat = w1_ref.shape[0]
    rows, wide = h_ref.shape
    queries = wide // feat
    send = ghost1.shape[0] // n_d
    e_in = ein_ref.shape[1]
    e_bd = ebd_ref.shape[1]
    half = red_all.shape[1] // CHUNK * CHUNK
    n_chunks = half // CHUNK

    barrier = pltpu.get_barrier_semaphore()

    def greet(i, carry):
        t = lax.rem(lin + i, total)
        pl.semaphore_signal(
            barrier, inc=1, device_id=(t // n_d, lax.rem(t, n_d)), device_id_type=MESH
        )
        return carry

    lax.fori_loop(1, total, greet, 0)

    def block_copy(phase, src, dst, size, i, send_to):
        peer = lax.rem(me_d + i, n_d)
        del send_to
        if size is None:
            s, d = src.at[peer], dst.at[me_d]
        else:
            s = src.at[pl.ds(pl.multiple_of(peer * size, size), size)]
            d = dst.at[pl.ds(pl.multiple_of(me_d * size, size), size)]
        return pltpu.make_async_remote_copy(
            src_ref=s,
            dst_ref=d,
            send_sem=xsend.at[phase, i],
            recv_sem=xrecv.at[phase, i],
            device_id=(me_q, peer),
            device_id_type=MESH,
        )

    def exchange_start(phase, src, dst, size):
        def go(i, carry):
            block_copy(phase, src, dst, size, i, True).start()
            return carry

        lax.fori_loop(1, n_d, go, 0)
        if size is None:
            dst[me_d] = src[me_d]
        else:
            own = pl.ds(pl.multiple_of(me_d * size, size), size)
            dst[own, :] = src[own, :]

    def exchange_wait(phase, src, dst, size):
        def go(i, carry):
            block_copy(phase, src, dst, size, i, False).wait()
            return carry

        lax.fori_loop(1, n_d, go, 0)

    def reducer(c):
        return (c * total) // n_chunks

    def rs_copy(layer, c):
        t = reducer(c)
        return t, pltpu.make_async_remote_copy(
            src_ref=red_src.at[layer, pl.ds(pl.multiple_of(c * CHUNK, CHUNK), CHUNK)],
            dst_ref=red_in.at[layer, lin],
            send_sem=rsend.at[layer, c],
            recv_sem=rrecv.at[layer, lin],
            device_id=(t // n_d, lax.rem(t, n_d)),
            device_id_type=MESH,
        )

    def rs_start(layer):
        def go(c, carry):
            t, copy = rs_copy(layer, c)

            @pl.when(t != lin)
            def _():
                copy.start()

            @pl.when(t == lin)
            def _():
                red_in[layer, lin] = red_src[
                    layer, pl.ds(pl.multiple_of(c * CHUNK, CHUNK), CHUNK), :
                ]

            return carry

        lax.fori_loop(0, n_chunks, go, 0)

    def ag_copy(layer, c, i):
        t = lax.rem(lin + i, total)
        return pltpu.make_async_remote_copy(
            src_ref=red_sum.at[layer],
            dst_ref=red_all.at[layer, pl.ds(pl.multiple_of(c * CHUNK, CHUNK), CHUNK)],
            send_sem=gsend.at[layer, i],
            recv_sem=grecv.at[layer, c],
            device_id=(t // n_d, lax.rem(t, n_d)),
            device_id_type=MESH,
        )

    def rs_finish_ag_start(layer):
        def each(c, carry):
            t, copy = rs_copy(layer, c)

            @pl.when(t != lin)
            def _():
                copy.wait_send()

            @pl.when(t == lin)
            def _():
                def take(i, acc):
                    s = lax.rem(lin + i, total)
                    pltpu.make_async_remote_copy(
                        src_ref=red_src.at[layer, pl.ds(0, CHUNK)],
                        dst_ref=red_in.at[layer, s],
                        send_sem=rsend.at[layer, 0],
                        recv_sem=rrecv.at[layer, s],
                        device_id=(s // n_d, lax.rem(s, n_d)),
                        device_id_type=MESH,
                    ).wait_recv()
                    return acc + red_in[layer, s]

                acc = lax.fori_loop(1, total, take, red_in[layer, lin])
                red_sum[layer] = acc
                red_all[layer, pl.ds(pl.multiple_of(c * CHUNK, CHUNK), CHUNK), :] = acc

                def put(i, carry2):
                    ag_copy(layer, c, i).start()
                    return carry2

                lax.fori_loop(1, total, put, 0)

            return carry

        lax.fori_loop(0, n_chunks, each, 0)

    def ag_finish(layer):
        def each(c, carry):
            t = reducer(c)

            @pl.when(t == lin)
            def _():
                def done(i, carry2):
                    ag_copy(layer, c, i).wait_send()
                    return carry2

                lax.fori_loop(1, total, done, 0)

            @pl.when(t != lin)
            def _():
                ag_copy(layer, c, 1).wait_recv()

            return carry

        lax.fori_loop(0, n_chunks, each, 0)

    def pack(layer, rg, wg):
        first = half
        rest = rel_rows - first
        red_src[layer, :, pl.ds(0, feat)] = rg[:first]
        red_src[layer, pl.ds(0, rest), pl.ds(feat, feat)] = rg[first:]
        red_src[layer, pl.ds(rest, feat), pl.ds(feat, feat)] = wg
        left = first - rest - feat
        if left:
            red_src[layer, pl.ds(rest + feat, left), pl.ds(feat, feat)] = jnp.zeros((left, feat), F32)

    def unpack(layer):
        first = half
        rest = rel_rows - first
        grel_ref[layer, pl.ds(0, first), :] = red_all[layer, :, pl.ds(0, feat)] * scale_r
        grel_ref[layer, pl.ds(first, rel_count - first), :] = (
            red_all[layer, pl.ds(0, rel_count - first), pl.ds(feat, feat)] * scale_r
        )
        gw_ref[layer] = red_all[layer, pl.ds(rest, feat), pl.ds(feat, feat)] * scale_w

    onehot_into(vt, ein_ref[1:2, :], 0, 64)
    onehot_into(vt, ebd_ref[1:2, :], e_in, 64)
    pl.semaphore_wait(barrier, total - 1)
    exchange_start(0, gs_ref, req, None)
    onehot_into(st_in, ein_ref[0:1, :], 0, 64)
    onehot_into(st_bd, ebd_ref[0:1, :], 0, 64)
    onehot_into(rt, ein_ref[2:3, :], 0, 32)
    onehot_into(rt, ebd_ref[2:3, :], e_in, 32)
    rel_e[...] = dot_nn(relt_ref[pl.ds(0, 2 * feat), :], rt[...]).astype(BF16)

    row_ids = lax.broadcasted_iota(jnp.int32, (feat, rows), 1) + me_d * rows
    lane_rel = lax.broadcasted_iota(jnp.int32, (feat, relt_ref.shape[1]), 1)
    qtab = relt_ref[pl.ds(2 * feat, feat), :].astype(F32)
    boost_parts = []
    for q in range(queries):
        vec = jnp.sum(jnp.where(lane_rel == qrel_ref[q], qtab, 0.0), axis=1, keepdims=True)
        boost_parts.append(jnp.where(row_ids == qhead_ref[q], vec, 0.0))
    boost = jnp.concatenate(boost_parts, axis=0)

    exchange_wait(0, gs_ref, req, None)
    per = 128 // send
    lane_group = lax.broadcasted_iota(jnp.int32, (1, 128), 1) // send
    wanted = []
    for j in range(n_d // per):
        vec = jnp.zeros((1, 128), jnp.int32)
        for k in range(per):
            vec = jnp.where(lane_group == k, req[j * per + k, 0:1, :], vec)
        wanted.append(vec)
    wanted = jnp.concatenate(wanted, axis=1)
    slot_ids = lax.broadcasted_iota(jnp.int32, (bnd_ref.shape[0], n_d * send), 0)
    owner = jnp.sum(jnp.where(slot_ids == wanted, bnd_ref[...], 0), axis=0, keepdims=True)
    own_ids = lax.broadcasted_iota(jnp.int32, (rows, n_d * send), 0)
    pick_t32 = jnp.where(own_ids == owner, 1.0, 0.0)
    pick_t = pick_t32.astype(BF16)
    pick = pick_t32.T.astype(BF16)

    out1[...] = dot_nn(pick, h_ref[...]).astype(BF16)
    exchange_start(1, out1, ghost1, send)

    h32 = h_ref[...].astype(F32)
    h_t32 = h32.T
    h_t = h_t32.astype(BF16)

    def rel_tile(layer, lo, count):
        part = rel_e[pl.ds(layer * feat, feat), pl.ds(lo, count)].astype(F32)
        return jnp.concatenate([part] * queries, axis=0)

    def aggregate(layer, table_t, onehot, save, lo, count):
        sourced = dot_nn(table_t, onehot[...])
        save[:, pl.ds(lo, count)] = sourced.astype(BF16)
        message = split_hi_lo(sourced * rel_tile(layer, lo, count), 0)
        both = dot_nt(message, vt[:, pl.ds(lo, count)])
        return both[:wide] + both[wide:]

    def normalise(summed, w_ref):
        summed_b = summed.astype(BF16)
        normed, rstds = [], []
        for q in range(queries):
            mixed = lax.dot_general(
                w_ref[...],
                summed_b[q * feat : (q + 1) * feat],
                (((0,), (0,)), ((), ())),
                preferred_element_type=F32,
            )
            center = mixed - jnp.mean(mixed, axis=0, keepdims=True)
            rstd = lax.rsqrt(jnp.mean(center * center, axis=0, keepdims=True) + 1e-05)
            normed.append(center * rstd)
            rstds.append(rstd)
        return summed_b, normed, rstds

    def back_layer(up_t, normed, rstds, summed_b, w_ref):
        wgrad = jnp.zeros((feat, feat), F32)
        dsum = []
        for q in range(queries):
            y = normed[q]
            sig = jax.nn.sigmoid(y)
            dact = up_t[q * feat : (q + 1) * feat] * sig * (1.0 + y * (1.0 - sig))
            dmix = rstds[q] * (
                dact
                - jnp.mean(dact, axis=0, keepdims=True)
                - y * jnp.mean(dact * y, axis=0, keepdims=True)
            )
            dmix_b = dmix.astype(BF16)
            wgrad = wgrad + dot_nt(summed_b[q * feat : (q + 1) * feat], dmix_b)
            dsum.append(dot_nn(w_ref[...], dmix_b).astype(BF16))
        return wgrad, jnp.concatenate(dsum, axis=0)

    def rel_grad(down, save):
        prod = down * save[...].astype(F32)
        tot = prod[:feat]
        for q in range(1, queries):
            tot = tot + prod[q * feat : (q + 1) * feat]
        both = dot_nt(rt[pl.ds(0, rel_rows), :], split_hi_lo(tot, 0))
        return both[:, :feat] + both[:, feat:]

    def table_grad(layer, down, onehot, lo, count):
        message = split_hi_lo(down[:, lo : lo + count] * rel_tile(layer, lo, count), 0)
        both = dot_nt(onehot[...], message)
        return both[:, :wide] + both[:, wide:]

    def give_back(ret_in):
        both = dot_nn(pick_t, split_hi_lo(ret_in[...], 1))
        return both[:, :wide] + both[:, wide:]

    sum1 = aggregate(0, h_t, st_in, x1, 0, e_in) + boost
    exchange_wait(1, out1, ghost1, send)
    sum1 = sum1 + aggregate(0, ghost1[...].astype(F32).T.astype(BF16), st_bd, x1, e_in, e_bd)
    sum1_b, norm1, rstd1 = normalise(sum1, w1_ref)
    h2_t = (
        jnp.concatenate([y * jax.nn.sigmoid(y) for y in norm1], axis=0) + h_t32
    ).astype(BF16)

    out2[...] = dot_nt(pick, h2_t).astype(BF16)
    exchange_start(2, out2, ghost2, send)
    sum2 = aggregate(1, h2_t, st_in, x2, 0, e_in) + boost
    exchange_wait(2, out2, ghost2, send)
    sum2 = sum2 + aggregate(1, ghost2[...].astype(F32).T.astype(BF16), st_bd, x2, e_in, e_bd)
    sum2_b, norm2, rstd2 = normalise(sum2, w2_ref)

    cot32 = cot_ref[...].astype(F32)
    wg2, dsum2 = back_layer(cot32.T, norm2, rstd2, sum2_b, w2_ref)
    down2 = dot_nn(dsum2, vt[...])
    ret_out2[...] = table_grad(1, down2, st_bd, e_in, e_bd)
    exchange_start(3, ret_out2, ret_in2, send)
    mid = cot32 + table_grad(1, down2, st_in, 0, e_in)
    pack(1, rel_grad(down2, x2), wg2)
    exchange_wait(3, ret_out2, ret_in2, send)
    rs_start(1)
    mid = mid + give_back(ret_in2)

    wg1, dsum1 = back_layer(mid.T, norm1, rstd1, sum1_b, w1_ref)
    down1 = dot_nn(dsum1, vt[...])
    rs_finish_ag_start(1)
    pack(0, rel_grad(down1, x1), wg1)
    rs_start(0)
    ret_out1[...] = table_grad(0, down1, st_bd, e_in, e_bd)
    exchange_start(4, ret_out1, ret_in1, send)
    base = mid + table_grad(0, down1, st_in, 0, e_in)
    rs_finish_ag_start(0)
    exchange_wait(4, ret_out1, ret_in1, send)
    gin_ref[...] = base + give_back(ret_in1)
    ag_finish(1)
    unpack(1)
    ag_finish(0)
    unpack(0)


def body(
    h_in,
    cotangent,
    w_one,
    w_two,
    rel_one,
    rel_two,
    query_emb,
    q_head,
    q_rel,
    bnd_rows,
    ghost_slots,
    edges_in,
    edges_bd,
):
    rows, wide = h_in.shape
    feat = w_one.shape[0]
    queries = wide // feat
    rel_count = rel_one.shape[0]
    n_d = lax.axis_size("dom")
    n_q = lax.axis_size("query")
    total = n_d * n_q
    send = ghost_slots.shape[1]
    ghosts = n_d * send
    e_in, e_bd = edges_in.shape[1], edges_bd.shape[1]
    edges = e_in + e_bd
    rel_pad = -(-(rel_count + 1) // 128) * 128
    rel_rows = -(-(rel_count + 1) // 16) * 16
    half = -(-((rel_rows + feat + 1) // 2) // CHUNK) * CHUNK
    n_chunks = half // CHUNK
    scale_w = 1.0 / math.sqrt(rows * n_d * queries * n_q)
    scale_r = math.sqrt(rel_count / (n_d * edges * queries * n_q))

    tables = jnp.concatenate([rel_one, rel_two, query_emb], axis=1)
    rel_t = jnp.pad(tables, ((0, rel_pad - rel_count), (0, 0))).T
    slots = jnp.broadcast_to(jnp.tile(ghost_slots, (1, 128 // send))[:, None, :], (n_d, 8, 128))

    vmem = pl.BlockSpec(memory_space=pltpu.VMEM)
    smem = pl.BlockSpec(memory_space=pltpu.SMEM)
    dma = pltpu.SemaphoreType.DMA
    return pl.pallas_call(
        functools.partial(kernel, n_q, n_d, scale_w, scale_r, rel_count, rel_rows),
        out_shape=(
            jax.ShapeDtypeStruct((rows, wide), F32),
            jax.ShapeDtypeStruct((2, feat, feat), F32),
            jax.ShapeDtypeStruct((2, rel_count, feat), F32),
        ),
        in_specs=[vmem] * 5 + [smem] * 2 + [vmem] * 4,
        out_specs=(vmem, vmem, vmem),
        scratch_shapes=[
            pltpu.VMEM((rel_pad, edges), BF16),
            pltpu.VMEM((rows, edges), BF16),
            pltpu.VMEM((rows, e_in), BF16),
            pltpu.VMEM((ghosts, e_bd), BF16),
            pltpu.VMEM((2 * feat, edges), BF16),
            pltpu.VMEM((wide, edges), BF16),
            pltpu.VMEM((wide, edges), BF16),
            pltpu.VMEM((n_d, 8, 128), jnp.int32),
            pltpu.VMEM((ghosts, wide), BF16),
            pltpu.VMEM((ghosts, wide), BF16),
            pltpu.VMEM((ghosts, wide), BF16),
            pltpu.VMEM((ghosts, wide), BF16),
            pltpu.VMEM((ghosts, wide), F32),
            pltpu.VMEM((ghosts, wide), F32),
            pltpu.VMEM((ghosts, wide), F32),
            pltpu.VMEM((ghosts, wide), F32),
            pltpu.VMEM((2, half, 2 * feat), F32),
            pltpu.VMEM((2, total, CHUNK, 2 * feat), F32),
            pltpu.VMEM((2, CHUNK, 2 * feat), F32),
            pltpu.VMEM((2, half, 2 * feat), F32),
            dma((5, n_d)),
            dma((5, n_d)),
            dma((2, n_chunks)),
            dma((2, total)),
            dma((2, total)),
            dma((2, n_chunks)),
        ],
        compiler_params=pltpu.CompilerParams(
            collective_id=0, has_side_effects=True, vmem_limit_bytes=48 * 1024 * 1024
        ),
    )(
        h_in,
        cotangent,
        w_one,
        w_two,
        rel_t,
        q_head,
        q_rel,
        bnd_rows[:, None],
        slots,
        edges_in,
        edges_bd,
    )


def solution(mesh):
    return jax.shard_map(
        body,
        mesh=mesh,
        in_specs=(
            P("dom", "query"),
            P("dom", "query"),
            P(),
            P(),
            P(),
            P(),
            P(),
            P("query"),
            P("query"),
            P("dom"),
            P("dom", None),
            P(None, "dom"),
            P(None, "dom"),
        ),
        out_specs=(P("dom", "query"), P(), P()),
        check_vma=False,
    )
```

profile of v0, /device:TPU:0, one launch (start us, length us, event | category | flops | bytes accessed | tf_op | source)
XLA Modules:
  0.0 59.5 jit_solution(4586991409504182869)
XLA Ops:
  0.6 0.0 copy-start.12
  0.6 0.0 copy-start.11
  0.7 0.6 %copy-done.12 = s32[64]{0:T(128)S(1)} copy-done((s32[64]{0:T(128)S(1)}, s32[64]{0:T(128)}, u32[]{:S(2)}) %copy-start.12) | copy-done | bytes 280
  1.3 0.0 copy-start.10
  1.3 0.1 copy.16.bnd_ref
  1.4 0.0 copy-done.11
  1.4 0.0 copy-start.9
  1.4 0.0 copy-start.8
  1.4 0.1 tile.9
  1.5 0.7 %copy-done.10 = bf16[535,64]{0,1:T(8,128)(2,1)S(1)} copy-done((bf16[535,64]{0,1:T(8,128)(2,1)S(1)}, bf16[535,64]{0,1:T(8,128)(2,1)}, u32[]{:S(2)}) %copy-start.10) | copy-done | bytes 68504
  2.2 0.1 copy-done.9
  2.3 0.0 copy-done.8
  2.3 0.0 copy-start
  2.3 0.0 copy-start.1
  2.3 0.0 copy-start.2
  2.3 0.0 copy-start.3
  2.3 0.0 copy-start.4
  2.4 0.0 copy-start.5
  2.4 0.0 copy-start.6
  2.4 0.0 copy-start.7
  2.4 0.7 %copy-done = bf16[256,128]{1,0:T(8,128)(2,1)S(1)} copy-done((bf16[256,128]{1,0:T(8,128)(2,1)S(1)}, bf16[256,128]{1,0:T(8,128)(2,1)}, u32[]{:S(2)}) %copy-start) | copy-done | bytes 65560
  3.2 0.0 copy-done.1
  3.2 0.0 copy-done.2
  3.2 0.0 copy-done.3
  3.2 0.0 copy-done.4
  3.2 0.0 copy-done.5
  3.2 0.0 copy-done.6
  3.2 0.0 copy-done.7
  3.2 54.1 %shard_map.148 = (f32[256,128]{1,0:T(8,128)S(1)}, f32[2,64,64]{2,1,0:T(8,128)S(1)}, f32[2,535,64]{2,1,0:T(8,128)S(1)}) custom-call(bf16[256,128]{1,0:T(8,128)(2,1)S(1)} %copy-done, bf16[256,128]{1,0:T(8,128)(2,1)S(1)} %copy-done.1, bf16[64,64]{1,0:T(8,128)(2,1)S(1)} %copy-done.2, bf16[64,64]{1,0:T(8,128)(2,1)S(1)} %copy-done.3, ...), custom_call_target="tpu_custom_call" | custom-call | tf_op jit(solution)/shard_map/pallas_call | solution.py:457
  57.3 0.9 %copy.17 = f32[2,535,64]{1,2,0:T(8,128)} copy(f32[2,535,64]{2,1,0:T(8,128)S(1)} %get-tuple-element.5) | data formatting | bytes 547840 | tf_op jit(solution)/shard_map/pallas_call | solution.py:457
  58.3 0.7 %copy.20 = f32[256,128]{1,0:T(8,128)} copy(f32[256,128]{1,0:T(8,128)S(1)} %get-tuple-element.9) | data formatting | bytes 262144
  58.9 0.6 %copy.21 = f32[2,64,64]{2,1,0:T(8,128)} copy(f32[2,64,64]{2,1,0:T(8,128)S(1)} %get-tuple-element.10) | data formatting | bytes 65536
  (3 shorter events, 0.1 us)
Async XLA Ops:
  0.6 0.7 %copy-start.12 = (s32[64]{0:T(128)S(1)}, s32[64]{0:T(128)}, u32[]{:S(2)}) copy-start(s32[64]{0:T(128)} %param.22) | copy-start | bytes 772
  0.6 0.7 %copy-start.11 = (s32[16,16]{1,0:T(8,128)S(1)}, s32[16,16]{1,0:T(8,128)}, u32[]{:S(2)}) copy-start(s32[16,16]{1,0:T(8,128)} %param.23) | copy-start | bytes 3076
  1.3 0.9 %copy-start.10 = (bf16[535,64]{0,1:T(8,128)(2,1)S(1)}, bf16[535,64]{0,1:T(8,128)(2,1)}, u32[]{:S(2)}) copy-start(bf16[535,64]{0,1:T(8,128)(2,1)} %param.17) | copy-start | bytes 205444
  1.4 0.9 %copy-start.9 = (bf16[535,64]{0,1:T(8,128)(2,1)S(1)}, bf16[535,64]{0,1:T(8,128)(2,1)}, u32[]{:S(2)}) copy-start(bf16[535,64]{0,1:T(8,128)(2,1)} %param.18) | copy-start | bytes 205444
  1.4 0.9 %copy-start.8 = (bf16[535,64]{0,1:T(8,128)(2,1)S(1)}, bf16[535,64]{0,1:T(8,128)(2,1)}, u32[]{:S(2)}) copy-start(bf16[535,64]{0,1:T(8,128)(2,1)} %param.19) | copy-start | bytes 205444
  2.3 0.8 %copy-start = (bf16[256,128]{1,0:T(8,128)(2,1)S(1)}, bf16[256,128]{1,0:T(8,128)(2,1)}, u32[]{:S(2)}) copy-start(bf16[256,128]{1,0:T(8,128)(2,1)} %h_ref.1) | copy-start | bytes 196612
  2.3 0.9 %copy-start.1 = (bf16[256,128]{1,0:T(8,128)(2,1)S(1)}, bf16[256,128]{1,0:T(8,128)(2,1)}, u32[]{:S(2)}) copy-start(bf16[256,128]{1,0:T(8,128)(2,1)} %cot_ref.1) | copy-start | bytes 196612
  2.3 0.9 %copy-start.2 = (bf16[64,64]{1,0:T(8,128)(2,1)S(1)}, bf16[64,64]{1,0:T(8,128)(2,1)}, u32[]{:S(2)}) copy-start(bf16[64,64]{1,0:T(8,128)(2,1)} %w1_ref.1) | copy-start | bytes 24580
  2.3 0.9 %copy-start.3 = (bf16[64,64]{1,0:T(8,128)(2,1)S(1)}, bf16[64,64]{1,0:T(8,128)(2,1)}, u32[]{:S(2)}) copy-start(bf16[64,64]{1,0:T(8,128)(2,1)} %w2_ref.1) | copy-start | bytes 24580
  2.3 0.9 %copy-start.4 = (s32[3,1024]{1,0:T(4,128)S(1)}, s32[3,1024]{1,0:T(4,128)}, u32[]{:S(2)}) copy-start(s32[3,1024]{1,0:T(4,128)} %ein_ref.1) | copy-start | bytes 36868
  2.4 0.9 %copy-start.5 = (s32[3,1024]{1,0:T(4,128)S(1)}, s32[3,1024]{1,0:T(4,128)}, u32[]{:S(2)}) copy-start(s32[3,1024]{1,0:T(4,128)} %ebd_ref.1) | copy-start | bytes 36868
  2.4 0.9 %copy-start.6 = (s32[2]{0:T(128)S(1)}, s32[2]{0:T(128)}, u32[]{:S(2)}) copy-start(s32[2]{0:T(128)} %qhead_ref.1) | copy-start | bytes 28
  2.4 0.8 %copy-start.7 = (s32[2]{0:T(128)S(1)}, s32[2]{0:T(128)}, u32[]{:S(2)}) copy-start(s32[2]{0:T(128)} %qrel_ref.1) | copy-start | bytes 28
where the time goes:
time: 59.8 us; the launch traced here: 59.5 us
  Pallas kernels  54.1 us (90%)
  local copies, waits for them, and re-layouts  4.69 us (8%)
  between operations  0.75 us (1%)
    pallas_call x1, Pallas kernels, body(): pl.pallas_call(functools.partial(kernel, n_q, n_d, scale_w, scale_r, rel_...  54.1 us
    unnamed x28, local copies, waits for them, and re-layouts  3.55 us

commit v1 on v0

--- a/solution.py
+++ b/solution.py
@@ -52,7 +52,9 @@
     cot_ref,
     w1_ref,
     w2_ref,
-    relt_ref,
+    r1_ref,
+    r2_ref,
+    qe_ref,
     qhead_ref,
     qrel_ref,
     bnd_ref,
@@ -62,6 +64,8 @@
     gin_ref,
     gw_ref,
     grel_ref,
+    relt,
+    gs_x,
     rt,
     vt,
     st_in,
@@ -99,8 +103,14 @@
     send = ghost1.shape[0] // n_d
     e_in = ein_ref.shape[1]
     e_bd = ebd_ref.shape[1]
-    half = red_all.shape[1] // CHUNK * CHUNK
-    n_chunks = half // CHUNK
+    lanes = red_all.shape[2] // 128
+    n_chunks = feat // CHUNK * lanes
+
+    def tile_of(c):
+        return (
+            pl.ds(pl.multiple_of(c // lanes * CHUNK, CHUNK), CHUNK),
+            pl.ds(pl.multiple_of(lax.rem(c, lanes) * 128, 128), 128),
+        )
 
     barrier = pltpu.get_barrier_semaphore()
 
@@ -149,13 +159,13 @@
 
         lax.fori_loop(1, n_d, go, 0)
 
-    def reducer(c):
-        return (c * total) // n_chunks
+    mine = (lin * n_chunks + total - 1) // total
+    adds = jnp.logical_and(mine < n_chunks, (mine * total) // n_chunks == lin)
 
     def rs_copy(layer, c):
-        t = reducer(c)
+        t = (c * total) // n_chunks
         return t, pltpu.make_async_remote_copy(
-            src_ref=red_src.at[layer, pl.ds(pl.multiple_of(c * CHUNK, CHUNK), CHUNK)],
+            src_ref=red_src.at[(layer, *tile_of(c))],
             dst_ref=red_in.at[layer, lin],
             send_sem=rsend.at[layer, c],
             recv_sem=rrecv.at[layer, lin],
@@ -171,12 +181,6 @@
             def _():
                 copy.start()
 
-            @pl.when(t == lin)
-            def _():
-                red_in[layer, lin] = red_src[
-                    layer, pl.ds(pl.multiple_of(c * CHUNK, CHUNK), CHUNK), :
-                ]
-
             return carry
 
         lax.fori_loop(0, n_chunks, go, 0)
@@ -185,7 +189,7 @@
         t = lax.rem(lin + i, total)
         return pltpu.make_async_remote_copy(
             src_ref=red_sum.at[layer],
-            dst_ref=red_all.at[layer, pl.ds(pl.multiple_of(c * CHUNK, CHUNK), CHUNK)],
+            dst_ref=red_all.at[(layer, *tile_of(c))],
             send_sem=gsend.at[layer, i],
             recv_sem=grecv.at[layer, c],
             device_id=(t // n_d, lax.rem(t, n_d)),
@@ -193,101 +197,92 @@
         )
 
     def rs_finish_ag_start(layer):
+        @pl.when(adds)
+        def _():
+            def take(i, acc):
+                s = lax.rem(lin + i, total)
+                pltpu.make_async_remote_copy(
+                    src_ref=red_src.at[(layer, *tile_of(0))],
+                    dst_ref=red_in.at[layer, s],
+                    send_sem=rsend.at[layer, 0],
+                    recv_sem=rrecv.at[layer, s],
+                    device_id=(s // n_d, lax.rem(s, n_d)),
+                    device_id_type=MESH,
+                ).wait_recv()
+                return acc + red_in[layer, s].astype(F32)
+
+            own = red_src[(layer, *tile_of(mine))].astype(F32)
+            acc = lax.fori_loop(1, total, take, own).astype(BF16)
+            red_sum[layer] = acc
+            red_all[(layer, *tile_of(mine))] = acc
+
+            def put(i, carry):
+                ag_copy(layer, mine, i).start()
+                return carry
+
+            lax.fori_loop(1, total, put, 0)
+
+    def ag_finish(layer):
         def each(c, carry):
             t, copy = rs_copy(layer, c)
 
             @pl.when(t != lin)
             def _():
                 copy.wait_send()
-
-            @pl.when(t == lin)
-            def _():
-                def take(i, acc):
-                    s = lax.rem(lin + i, total)
-                    pltpu.make_async_remote_copy(
-                        src_ref=red_src.at[layer, pl.ds(0, CHUNK)],
-                        dst_ref=red_in.at[layer, s],
-                        send_sem=rsend.at[layer, 0],
-                        recv_sem=rrecv.at[layer, s],
-                        device_id=(s // n_d, lax.rem(s, n_d)),
-                        device_id_type=MESH,
-                    ).wait_recv()
-                    return acc + red_in[layer, s]
-
-                acc = lax.fori_loop(1, total, take, red_in[layer, lin])
-                red_sum[layer] = acc
-                red_all[layer, pl.ds(pl.multiple_of(c * CHUNK, CHUNK), CHUNK), :] = acc
-
-                def put(i, carry2):
-                    ag_copy(layer, c, i).start()
-                    return carry2
-
-                lax.fori_loop(1, total, put, 0)
+                ag_copy(layer, c, 1).wait_recv()
 
             return carry
 
         lax.fori_loop(0, n_chunks, each, 0)
 
-    def ag_finish(layer):
-        def each(c, carry):
-            t = reducer(c)
-
-            @pl.when(t == lin)
-            def _():
-                def done(i, carry2):
-                    ag_copy(layer, c, i).wait_send()
-                    return carry2
-
-                lax.fori_loop(1, total, done, 0)
-
-            @pl.when(t != lin)
-            def _():
-                ag_copy(layer, c, 1).wait_recv()
-
-            return carry
-
-        lax.fori_loop(0, n_chunks, each, 0)
+        @pl.when(adds)
+        def _():
+            def done(i, carry):
+                ag_copy(layer, mine, i).wait_send()
+                return carry
+
+            lax.fori_loop(1, total, done, 0)
 
     def pack(layer, rg, wg):
-        first = half
-        rest = rel_rows - first
-        red_src[layer, :, pl.ds(0, feat)] = rg[:first]
-        red_src[layer, pl.ds(0, rest), pl.ds(feat, feat)] = rg[first:]
-        red_src[layer, pl.ds(rest, feat), pl.ds(feat, feat)] = wg
-        left = first - rest - feat
+        parts = [rg, wg]
+        left = lanes * 128 - rel_rows - feat
         if left:
-            red_src[layer, pl.ds(rest + feat, left), pl.ds(feat, feat)] = jnp.zeros((left, feat), F32)
+            parts.append(jnp.zeros((feat, left), F32))
+        red_src[layer] = jnp.concatenate(parts, axis=1).astype(BF16)
 
     def unpack(layer):
-        first = half
-        rest = rel_rows - first
-        grel_ref[layer, pl.ds(0, first), :] = red_all[layer, :, pl.ds(0, feat)] * scale_r
-        grel_ref[layer, pl.ds(first, rel_count - first), :] = (
-            red_all[layer, pl.ds(0, rel_count - first), pl.ds(feat, feat)] * scale_r
-        )
-        gw_ref[layer] = red_all[layer, pl.ds(rest, feat), pl.ds(feat, feat)] * scale_w
+        summed = red_all[layer].astype(F32)
+        grel_ref[layer] = summed[:, :rel_count] * scale_r
+        gw_ref[layer] = summed[:, rel_rows : rel_rows + feat] * scale_w
+
+    per = 128 // send
+    spread = jnp.concatenate([gs_ref[...]] * per, axis=1)
+    for p in range(n_d):
+        gs_x[p] = spread[p : p + 1, :]
 
     onehot_into(vt, ein_ref[1:2, :], 0, 64)
     onehot_into(vt, ebd_ref[1:2, :], e_in, 64)
     pl.semaphore_wait(barrier, total - 1)
-    exchange_start(0, gs_ref, req, None)
+    exchange_start(0, gs_x, req, None)
     onehot_into(st_in, ein_ref[0:1, :], 0, 64)
     onehot_into(st_bd, ebd_ref[0:1, :], 0, 64)
     onehot_into(rt, ein_ref[2:3, :], 0, 32)
     onehot_into(rt, ebd_ref[2:3, :], e_in, 32)
-    rel_e[...] = dot_nn(relt_ref[pl.ds(0, 2 * feat), :], rt[...]).astype(BF16)
+    relt[...] = jnp.zeros_like(relt)
+    relt[pl.ds(0, feat), pl.ds(0, rel_count)] = r1_ref[...]
+    relt[pl.ds(feat, feat), pl.ds(0, rel_count)] = r2_ref[...]
+    rel_e[...] = dot_nn(relt[...], rt[...]).astype(BF16)
 
     row_ids = lax.broadcasted_iota(jnp.int32, (feat, rows), 1) + me_d * rows
-    lane_rel = lax.broadcasted_iota(jnp.int32, (feat, relt_ref.shape[1]), 1)
-    qtab = relt_ref[pl.ds(2 * feat, feat), :].astype(F32)
+    lane_rel = lax.broadcasted_iota(jnp.int32, (feat, rel_count), 1)
+    qtab = qe_ref[...].astype(F32)
     boost_parts = []
     for q in range(queries):
         vec = jnp.sum(jnp.where(lane_rel == qrel_ref[q], qtab, 0.0), axis=1, keepdims=True)
         boost_parts.append(jnp.where(row_ids == qhead_ref[q], vec, 0.0))
     boost = jnp.concatenate(boost_parts, axis=0)
 
-    exchange_wait(0, gs_ref, req, None)
-    per = 128 // send
+    exchange_wait(0, gs_x, req, None)
     lane_group = lax.broadcasted_iota(jnp.int32, (1, 128), 1) // send
     wanted = []
     for j in range(n_d // per):
@@ -296,10 +291,11 @@
             vec = jnp.where(lane_group == k, req[j * per + k, 0:1, :], vec)
         wanted.append(vec)
     wanted = jnp.concatenate(wanted, axis=1)
-    slot_ids = lax.broadcasted_iota(jnp.int32, (bnd_ref.shape[0], n_d * send), 0)
-    owner = jnp.sum(jnp.where(slot_ids == wanted, bnd_ref[...], 0), axis=0, keepdims=True)
-    own_ids = lax.broadcasted_iota(jnp.int32, (rows, n_d * send), 0)
-    pick_t32 = jnp.where(own_ids == owner, 1.0, 0.0)
+    slots = bnd_ref.shape[1]
+    slot_ids = lax.broadcasted_iota(jnp.int32, (slots, n_d * send), 0)
+    own_ids = lax.broadcasted_iota(jnp.int32, (rows, slots), 0)
+    row_of = jnp.where(own_ids == bnd_ref[...], 1.0, 0.0).astype(BF16)
+    pick_t32 = dot_nn(row_of, jnp.where(slot_ids == wanted, 1.0, 0.0).astype(BF16))
     pick_t = pick_t32.astype(BF16)
     pick = pick_t32.T.astype(BF16)
 
@@ -359,8 +355,8 @@
         tot = prod[:feat]
         for q in range(1, queries):
             tot = tot + prod[q * feat : (q + 1) * feat]
-        both = dot_nt(rt[pl.ds(0, rel_rows), :], split_hi_lo(tot, 0))
-        return both[:, :feat] + both[:, feat:]
+        both = dot_nt(split_hi_lo(tot, 0), rt[pl.ds(0, rel_rows), :])
+        return both[:feat] + both[feat:]
 
     def table_grad(layer, down, onehot, lo, count):
         message = split_hi_lo(down[:, lo : lo + count] * rel_tile(layer, lo, count), 0)
@@ -368,8 +364,7 @@
         return both[:, :wide] + both[:, wide:]
 
     def give_back(ret_in):
-        both = dot_nn(pick_t, split_hi_lo(ret_in[...], 1))
-        return both[:, :wide] + both[:, wide:]
+        return dot_nn(pick_t, ret_in[...])
 
     sum1 = aggregate(0, h_t, st_in, x1, 0, e_in) + boost
     exchange_wait(1, out1, ghost1, send)
@@ -389,7 +384,7 @@
     cot32 = cot_ref[...].astype(F32)
     wg2, dsum2 = back_layer(cot32.T, norm2, rstd2, sum2_b, w2_ref)
     down2 = dot_nn(dsum2, vt[...])
-    ret_out2[...] = table_grad(1, down2, st_bd, e_in, e_bd)
+    ret_out2[...] = table_grad(1, down2, st_bd, e_in, e_bd).astype(BF16)
     exchange_start(3, ret_out2, ret_in2, send)
     mid = cot32 + table_grad(1, down2, st_in, 0, e_in)
     pack(1, rel_grad(down2, x2), wg2)
@@ -399,11 +394,11 @@
 
     wg1, dsum1 = back_layer(mid.T, norm1, rstd1, sum1_b, w1_ref)
     down1 = dot_nn(dsum1, vt[...])
-    rs_finish_ag_start(1)
     pack(0, rel_grad(down1, x1), wg1)
     rs_start(0)
-    ret_out1[...] = table_grad(0, down1, st_bd, e_in, e_bd)
+    ret_out1[...] = table_grad(0, down1, st_bd, e_in, e_bd).astype(BF16)
     exchange_start(4, ret_out1, ret_in1, send)
+    rs_finish_ag_start(1)
     base = mid + table_grad(0, down1, st_in, 0, e_in)
     rs_finish_ag_start(0)
     exchange_wait(4, ret_out1, ret_in1, send)
@@ -442,28 +437,26 @@
     edges = e_in + e_bd
     rel_pad = -(-(rel_count + 1) // 128) * 128
     rel_rows = -(-(rel_count + 1) // 16) * 16
-    half = -(-((rel_rows + feat + 1) // 2) // CHUNK) * CHUNK
-    n_chunks = half // CHUNK
+    width = -(-(rel_rows + feat) // 128) * 128
+    n_chunks = feat // CHUNK * (width // 128)
     scale_w = 1.0 / math.sqrt(rows * n_d * queries * n_q)
     scale_r = math.sqrt(rel_count / (n_d * edges * queries * n_q))
-
-    tables = jnp.concatenate([rel_one, rel_two, query_emb], axis=1)
-    rel_t = jnp.pad(tables, ((0, rel_pad - rel_count), (0, 0))).T
-    slots = jnp.broadcast_to(jnp.tile(ghost_slots, (1, 128 // send))[:, None, :], (n_d, 8, 128))
 
     vmem = pl.BlockSpec(memory_space=pltpu.VMEM)
     smem = pl.BlockSpec(memory_space=pltpu.SMEM)
     dma = pltpu.SemaphoreType.DMA
-    return pl.pallas_call(
+    grad_in, grad_w, grad_rel_t = pl.pallas_call(
         functools.partial(kernel, n_q, n_d, scale_w, scale_r, rel_count, rel_rows),
         out_shape=(
             jax.ShapeDtypeStruct((rows, wide), F32),
             jax.ShapeDtypeStruct((2, feat, feat), F32),
-            jax.ShapeDtypeStruct((2, rel_count, feat), F32),
+            jax.ShapeDtypeStruct((2, feat, rel_count), F32),
         ),
-        in_specs=[vmem] * 5 + [smem] * 2 + [vmem] * 4,
+        in_specs=[vmem] * 7 + [smem] * 2 + [vmem] * 4,
         out_specs=(vmem, vmem, vmem),
         scratch_shapes=[
+            pltpu.VMEM((2 * feat, rel_pad), BF16),
+            pltpu.VMEM((n_d, 1, 128), jnp.int32),
             pltpu.VMEM((rel_pad, edges), BF16),
             pltpu.VMEM((rows, edges), BF16),
             pltpu.VMEM((rows, e_in), BF16),
@@ -471,19 +464,19 @@
             pltpu.VMEM((2 * feat, edges), BF16),
             pltpu.VMEM((wide, edges), BF16),
             pltpu.VMEM((wide, edges), BF16),
-            pltpu.VMEM((n_d, 8, 128), jnp.int32),
-            pltpu.VMEM((ghosts, wide), BF16),
-            pltpu.VMEM((ghosts, wide), BF16),
-            pltpu.VMEM((ghosts, wide), BF16),
-            pltpu.VMEM((ghosts, wide), BF16),
-            pltpu.VMEM((ghosts, wide), F32),
-            pltpu.VMEM((ghosts, wide), F32),
-            pltpu.VMEM((ghosts, wide), F32),
-            pltpu.VMEM((ghosts, wide), F32),
-            pltpu.VMEM((2, half, 2 * feat), F32),
-            pltpu.VMEM((2, total, CHUNK, 2 * feat), F32),
-            pltpu.VMEM((2, CHUNK, 2 * feat), F32),
-            pltpu.VMEM((2, half, 2 * feat), F32),
+            pltpu.VMEM((n_d, 1, 128), jnp.int32),
+            pltpu.VMEM((ghosts, wide), BF16),
+            pltpu.VMEM((ghosts, wide), BF16),
+            pltpu.VMEM((ghosts, wide), BF16),
+            pltpu.VMEM((ghosts, wide), BF16),
+            pltpu.VMEM((ghosts, wide), BF16),
+            pltpu.VMEM((ghosts, wide), BF16),
+            pltpu.VMEM((ghosts, wide), BF16),
+            pltpu.VMEM((ghosts, wide), BF16),
+            pltpu.VMEM((2, feat, width), BF16),
+            pltpu.VMEM((2, total, CHUNK, 128), BF16),
+            pltpu.VMEM((2, CHUNK, 128), BF16),
+            pltpu.VMEM((2, feat, width), BF16),
             dma((5, n_d)),
             dma((5, n_d)),
             dma((2, n_chunks)),
@@ -499,14 +492,17 @@
         cotangent,
         w_one,
         w_two,
-        rel_t,
+        rel_one.T,
+        rel_two.T,
+        query_emb.T,
         q_head,
         q_rel,
-        bnd_rows[:, None],
-        slots,
+        bnd_rows[None, :],
+        ghost_slots,
         edges_in,
         edges_bd,
     )
+    return grad_in, grad_w, jnp.swapaxes(grad_rel_t, 1, 2)
 
 
 def solution(mesh):

time: 59.8 us -> 54.9 us (0.918)
  Pallas kernels: 54.1 us -> 43 us
  local copies, waits for them, and re-layouts: 4.69 us -> 10.6 us
    pallas_call x1, Pallas kernels: 54.1 us -> 43 us  [body(): pl.pallas_call(functools.partial(kernel, n_q, n_d, scale_w, scale_r, rel_...]
    unnamed x28 -> x29, local copies, waits for them, and re-layouts: 3.55 us -> 10.6 us
    pallas_call x1 -> x0, local copies, waits for them, and re-layouts: 0.94 us -> none  [body(): pl.pallas_call(functools.partial(kernel, n_q, n_d, scale_w, scale_r, rel_...]
where the time goes in v1:
time: 54.9 us; the launch traced here: 54.2 us
  Pallas kernels  43 us (78%)
  local copies, waits for them, and re-layouts  10.6 us (19%)
  between operations  0.68 us (1%)
    pallas_call x1, Pallas kernels, body(): pl.pallas_call(functools.partial(kernel, n_q, n_d, scale_w, scale_r, rel_...  43 us
    unnamed x29, local copies, waits for them, and re-layouts  10.6 us

profile of v1, /device:TPU:0, one launch (start us, length us, event | category | flops | bytes accessed | tf_op | source)
XLA Modules:
  0.0 54.2 jit_solution(5974689679690566888)
XLA Ops:
  0.6 0.0 copy-start.10
  0.6 0.0 copy-start.11
  0.7 0.0 copy-start.12
  0.7 0.6 %copy-done.10 = s32[2]{0:T(128)S(1)} copy-done((s32[2]{0:T(128)S(1)}, s32[2]{0:T(128)}, u32[]{:S(2)}) %copy-start.10) | copy-done | bytes 32
  1.3 0.0 copy-done.11
  1.3 0.0 copy-done.12
  1.3 0.0 copy-start
  1.3 0.9 %copy-done = bf16[535,64]{0,1:T(8,128)(2,1)S(1)} copy-done((bf16[535,64]{0,1:T(8,128)(2,1)S(1)}, bf16[535,64]{0,1:T(8,128)(2,1)}, u32[]{:S(2)}) %copy-start) | copy-done | bytes 68504
  2.2 0.0 copy-start.1
  2.2 0.9 %copy-done.1 = bf16[535,64]{0,1:T(8,128)(2,1)S(1)} copy-done((bf16[535,64]{0,1:T(8,128)(2,1)S(1)}, bf16[535,64]{0,1:T(8,128)(2,1)}, u32[]{:S(2)}) %copy-start.1) | copy-done | bytes 68504
  3.1 0.0 copy-start.2
  3.1 0.9 %copy-done.2 = bf16[535,64]{0,1:T(8,128)(2,1)S(1)} copy-done((bf16[535,64]{0,1:T(8,128)(2,1)S(1)}, bf16[535,64]{0,1:T(8,128)(2,1)}, u32[]{:S(2)}) %copy-start.2) | copy-done | bytes 68504
  4.0 0.0 copy-start.3
  4.0 0.8 %copy-done.3 = bf16[256,128]{1,0:T(8,128)(2,1)S(1)} copy-done((bf16[256,128]{1,0:T(8,128)(2,1)S(1)}, bf16[256,128]{1,0:T(8,128)(2,1)}, u32[]{:S(2)}) %copy-start.3) | copy-done | bytes 65560
  4.8 0.0 copy-start.4
  4.8 0.8 %copy-done.4 = bf16[256,128]{1,0:T(8,128)(2,1)S(1)} copy-done((bf16[256,128]{1,0:T(8,128)(2,1)S(1)}, bf16[256,128]{1,0:T(8,128)(2,1)}, u32[]{:S(2)}) %copy-start.4) | copy-done | bytes 65560
  5.7 0.0 copy-start.5
  5.7 0.7 %copy-done.5 = bf16[64,64]{1,0:T(8,128)(2,1)S(1)} copy-done((bf16[64,64]{1,0:T(8,128)(2,1)S(1)}, bf16[64,64]{1,0:T(8,128)(2,1)}, u32[]{:S(2)}) %copy-start.5) | copy-done | bytes 8216
  6.4 0.0 copy-start.6
  6.4 0.7 %copy-done.6 = bf16[64,64]{1,0:T(8,128)(2,1)S(1)} copy-done((bf16[64,64]{1,0:T(8,128)(2,1)S(1)}, bf16[64,64]{1,0:T(8,128)(2,1)}, u32[]{:S(2)}) %copy-start.6) | copy-done | bytes 8216
  7.1 0.0 copy-start.7
  7.1 0.7 %copy-done.7 = s32[3,1024]{1,0:T(4,128)S(1)} copy-done((s32[3,1024]{1,0:T(4,128)S(1)}, s32[3,1024]{1,0:T(4,128)}, u32[]{:S(2)}) %copy-start.7) | copy-done | bytes 12312
  7.8 0.0 copy-start.8
  7.8 0.7 %copy-done.8 = s32[3,1024]{1,0:T(4,128)S(1)} copy-done((s32[3,1024]{1,0:T(4,128)S(1)}, s32[3,1024]{1,0:T(4,128)}, u32[]{:S(2)}) %copy-start.8) | copy-done | bytes 12312
  8.5 0.0 copy-start.9
  8.5 0.7 %copy-done.9 = s32[16,16]{1,0:T(8,128)S(1)} copy-done((s32[16,16]{1,0:T(8,128)S(1)}, s32[16,16]{1,0:T(8,128)}, u32[]{:S(2)}) %copy-start.9) | copy-done | bytes 1048
  9.2 43.0 %shard_map.148 = (f32[256,128]{1,0:T(8,128)S(1)}, f32[2,64,64]{2,1,0:T(8,128)S(1)}, f32[2,64,535]{2,1,0:T(8,128)S(1)}) custom-call(bf16[256,128]{1,0:T(8,128)(2,1)S(1)} %copy-done.3, bf16[256,128]{1,0:T(8,128)(2,1)S(1)} %copy-done.4, bf16[64,64]{1,0:T(8,128)(2,1)S(1)} %copy-done.5, bf16[64,64]{1,0:T(8,128)(2,1)S(1)} %copy-done.6, ...), custom_call_target="tpu_custom_call" | custom-call | tf_op jit(solution)/shard_map/pallas_call | solution.py:448
  52.2 0.7 %copy.19 = f32[256,128]{1,0:T(8,128)} copy(f32[256,128]{1,0:T(8,128)S(1)} %get-tuple-element.12) | data formatting | bytes 262144
  52.9 0.6 %copy.20 = f32[2,64,64]{2,1,0:T(8,128)} copy(f32[2,64,64]{2,1,0:T(8,128)S(1)} %get-tuple-element.13) | data formatting | bytes 65536
  53.5 0.7 %copy.21 = f32[2,535,64]{1,2,0:T(8,128)} copy(f32[2,535,64]{1,2,0:T(8,128)S(1)} %bitcast.5) | data formatting | bytes 547840
Async XLA Ops:
  0.6 0.7 %copy-start.10 = (s32[2]{0:T(128)S(1)}, s32[2]{0:T(128)}, u32[]{:S(2)}) copy-start(s32[2]{0:T(128)} %qhead_ref.1) | copy-start | bytes 28
  0.6 0.7 %copy-start.11 = (s32[2]{0:T(128)S(1)}, s32[2]{0:T(128)}, u32[]{:S(2)}) copy-start(s32[2]{0:T(128)} %qrel_ref.1) | copy-start | bytes 28
  0.7 0.7 %copy-start.12 = (s32[64]{0:T(128)S(1)}, s32[64]{0:T(128)}, u32[]{:S(2)}) copy-start(s32[64]{0:T(128)} %param.22) | copy-start | bytes 772
  1.3 0.9 %copy-start = (bf16[535,64]{0,1:T(8,128)(2,1)S(1)}, bf16[535,64]{0,1:T(8,128)(2,1)}, u32[]{:S(2)}) copy-start(bf16[535,64]{0,1:T(8,128)(2,1)} %param.17) | copy-start | bytes 205444
  2.2 0.9 %copy-start.1 = (bf16[535,64]{0,1:T(8,128)(2,1)S(1)}, bf16[535,64]{0,1:T(8,128)(2,1)}, u32[]{:S(2)}) copy-start(bf16[535,64]{0,1:T(8,128)(2,1)} %param.18) | copy-start | bytes 205444
  3.1 0.9 %copy-start.2 = (bf16[535,64]{0,1:T(8,128)(2,1)S(1)}, bf16[535,64]{0,1:T(8,128)(2,1)}, u32[]{:S(2)}) copy-start(bf16[535,64]{0,1:T(8,128)(2,1)} %param.19) | copy-start | bytes 205444
  4.0 0.8 %copy-start.3 = (bf16[256,128]{1,0:T(8,128)(2,1)S(1)}, bf16[256,128]{1,0:T(8,128)(2,1)}, u32[]{:S(2)}) copy-start(bf16[256,128]{1,0:T(8,128)(2,1)} %h_ref.1) | copy-start | bytes 196612
  4.8 0.8 %copy-start.4 = (bf16[256,128]{1,0:T(8,128)(2,1)S(1)}, bf16[256,128]{1,0:T(8,128)(2,1)}, u32[]{:S(2)}) copy-start(bf16[256,128]{1,0:T(8,128)(2,1)} %cot_ref.1) | copy-start | bytes 196612
  5.7 0.7 %copy-start.5 = (bf16[64,64]{1,0:T(8,128)(2,1)S(1)}, bf16[64,64]{1,0:T(8,128)(2,1)}, u32[]{:S(2)}) copy-start(bf16[64,64]{1,0:T(8,128)(2,1)} %w1_ref.1) | copy-start | bytes 24580
  6.4 0.7 %copy-start.6 = (bf16[64,64]{1,0:T(8,128)(2,1)S(1)}, bf16[64,64]{1,0:T(8,128)(2,1)}, u32[]{:S(2)}) copy-start(bf16[64,64]{1,0:T(8,128)(2,1)} %w2_ref.1) | copy-start | bytes 24580
  7.1 0.7 %copy-start.7 = (s32[3,1024]{1,0:T(4,128)S(1)}, s32[3,1024]{1,0:T(4,128)}, u32[]{:S(2)}) copy-start(s32[3,1024]{1,0:T(4,128)} %ein_ref.1) | copy-start | bytes 36868
  7.8 0.7 %copy-start.8 = (s32[3,1024]{1,0:T(4,128)S(1)}, s32[3,1024]{1,0:T(4,128)}, u32[]{:S(2)}) copy-start(s32[3,1024]{1,0:T(4,128)} %ebd_ref.1) | copy-start | bytes 36868
  8.5 0.7 %copy-start.9 = (s32[16,16]{1,0:T(8,128)S(1)}, s32[16,16]{1,0:T(8,128)}, u32[]{:S(2)}) copy-start(s32[16,16]{1,0:T(8,128)} %gs_ref.1) | copy-start | bytes 3076

commit v2 on v1

--- a/solution.py
+++ b/solution.py
@@ -39,6 +39,26 @@
         return carry
 
     lax.fori_loop(0, rows // block, fill, 0)
+
+
+def loop(low, high, step):
+    if high - low <= 32:
+        for i in range(low, high):
+            step(i, 0)
+    else:
+        lax.fori_loop(low, high, step, 0)
+
+
+def div(a, b):
+    return a // b if isinstance(a, int) else lax.div(a, b)
+
+
+def rem(a, b):
+    return a % b if isinstance(a, int) else lax.rem(a, b)
+
+
+def aligned(a, b):
+    return a if isinstance(a, int) else pl.multiple_of(a, b)
 
 
 def kernel(
@@ -48,22 +68,16 @@
     scale_r,
     rel_count,
     rel_rows,
-    h_ref,
-    cot_ref,
-    w1_ref,
-    w2_ref,
-    r1_ref,
-    r2_ref,
-    qe_ref,
-    qhead_ref,
-    qrel_ref,
-    bnd_ref,
-    gs_ref,
-    ein_ref,
-    ebd_ref,
-    gin_ref,
-    gw_ref,
-    grel_ref,
+    *refs,
+):
+    n_in = 13
+    hbm = refs[:n_in]
+    gin_ref, gw_ref, grel_ref = refs[n_in : n_in + 3]
+    local = refs[n_in + 3 : 2 * n_in + 3]
+    (
+        h_ref, cot_ref, w1_ref, w2_ref, r1_ref, r2_ref, qe_ref, qhead_ref, qrel_ref, bnd_ref, gs_ref, ein_ref, ebd_ref,
+    ) = local
+    (
     relt,
     gs_x,
     rt,
@@ -92,7 +106,8 @@
     rrecv,
     gsend,
     grecv,
-):
+    load_sem,
+    ) = refs[2 * n_in + 3 :]
     me_d = lax.axis_index("dom")
     me_q = lax.axis_index("query")
     total = n_q * n_d
@@ -108,8 +123,8 @@
 
     def tile_of(c):
         return (
-            pl.ds(pl.multiple_of(c // lanes * CHUNK, CHUNK), CHUNK),
-            pl.ds(pl.multiple_of(lax.rem(c, lanes) * 128, 128), 128),
+            pl.ds(aligned(div(c, lanes) * CHUNK, CHUNK), CHUNK),
+            pl.ds(aligned(rem(c, lanes) * 128, 128), 128),
         )
 
     barrier = pltpu.get_barrier_semaphore()
@@ -117,11 +132,19 @@
     def greet(i, carry):
         t = lax.rem(lin + i, total)
         pl.semaphore_signal(
-            barrier, inc=1, device_id=(t // n_d, lax.rem(t, n_d)), device_id_type=MESH
+            barrier, inc=1, device_id=(div(t, n_d), rem(t, n_d)), device_id_type=MESH
         )
         return carry
 
-    lax.fori_loop(1, total, greet, 0)
+    loop(1, total, greet)
+    loads = [
+        pltpu.make_async_copy(src, dst, load_sem.at[k])
+        for k, (src, dst) in enumerate(zip(hbm, local))
+    ]
+    for load in loads:
+        load.start()
+    for load in loads:
+        load.wait()
 
     def block_copy(phase, src, dst, size, i, send_to):
         peer = lax.rem(me_d + i, n_d)
@@ -145,7 +168,7 @@
             block_copy(phase, src, dst, size, i, True).start()
             return carry
 
-        lax.fori_loop(1, n_d, go, 0)
+        loop(1, n_d, go)
         if size is None:
             dst[me_d] = src[me_d]
         else:
@@ -157,19 +180,19 @@
             block_copy(phase, src, dst, size, i, False).wait()
             return carry
 
-        lax.fori_loop(1, n_d, go, 0)
+        loop(1, n_d, go)
 
     mine = (lin * n_chunks + total - 1) // total
     adds = jnp.logical_and(mine < n_chunks, (mine * total) // n_chunks == lin)
 
     def rs_copy(layer, c):
-        t = (c * total) // n_chunks
+        t = div(c * total, n_chunks)
         return t, pltpu.make_async_remote_copy(
             src_ref=red_src.at[(layer, *tile_of(c))],
             dst_ref=red_in.at[layer, lin],
             send_sem=rsend.at[layer, c],
             recv_sem=rrecv.at[layer, lin],
-            device_id=(t // n_d, lax.rem(t, n_d)),
+            device_id=(div(t, n_d), rem(t, n_d)),
             device_id_type=MESH,
         )
 
@@ -183,7 +206,7 @@
 
             return carry
 
-        lax.fori_loop(0, n_chunks, go, 0)
+        loop(0, n_chunks, go)
 
     def ag_copy(layer, c, i):
         t = lax.rem(lin + i, total)
@@ -192,27 +215,28 @@
             dst_ref=red_all.at[(layer, *tile_of(c))],
             send_sem=gsend.at[layer, i],
             recv_sem=grecv.at[layer, c],
-            device_id=(t // n_d, lax.rem(t, n_d)),
+            device_id=(div(t, n_d), rem(t, n_d)),
             device_id_type=MESH,
         )
 
     def rs_finish_ag_start(layer):
         @pl.when(adds)
         def _():
-            def take(i, acc):
+            def take(i, carry):
                 s = lax.rem(lin + i, total)
                 pltpu.make_async_remote_copy(
                     src_ref=red_src.at[(layer, *tile_of(0))],
                     dst_ref=red_in.at[layer, s],
                     send_sem=rsend.at[layer, 0],
                     recv_sem=rrecv.at[layer, s],
-                    device_id=(s // n_d, lax.rem(s, n_d)),
+                    device_id=(div(s, n_d), rem(s, n_d)),
                     device_id_type=MESH,
                 ).wait_recv()
-                return acc + red_in[layer, s].astype(F32)
-
-            own = red_src[(layer, *tile_of(mine))].astype(F32)
-            acc = lax.fori_loop(1, total, take, own).astype(BF16)
+                return carry
+
+            loop(1, total, take)
+            red_in[layer, lin] = red_src[(layer, *tile_of(mine))]
+            acc = jnp.sum(red_in[layer].astype(F32), axis=0).astype(BF16)
             red_sum[layer] = acc
             red_all[(layer, *tile_of(mine))] = acc
 
@@ -220,7 +244,7 @@
                 ag_copy(layer, mine, i).start()
                 return carry
 
-            lax.fori_loop(1, total, put, 0)
+            loop(1, total, put)
 
     def ag_finish(layer):
         def each(c, carry):
@@ -233,7 +257,7 @@
 
             return carry
 
-        lax.fori_loop(0, n_chunks, each, 0)
+        loop(0, n_chunks, each)
 
         @pl.when(adds)
         def _():
@@ -241,7 +265,7 @@
                 ag_copy(layer, mine, i).wait_send()
                 return carry
 
-            lax.fori_loop(1, total, done, 0)
+            loop(1, total, done)
 
     def pack(layer, rg, wg):
         parts = [rg, wg]
@@ -407,6 +431,15 @@
     unpack(1)
     ag_finish(0)
     unpack(0)
+
+
+def write_out(*refs):
+    sems = refs[6]
+    copies = [pltpu.make_async_copy(refs[k], refs[3 + k], sems.at[k]) for k in range(3)]
+    for copy in copies:
+        copy.start()
+    for copy in copies:
+        copy.wait()
 
 
 def body(
@@ -442,52 +475,7 @@
     scale_w = 1.0 / math.sqrt(rows * n_d * queries * n_q)
     scale_r = math.sqrt(rel_count / (n_d * edges * queries * n_q))
 
-    vmem = pl.BlockSpec(memory_space=pltpu.VMEM)
-    smem = pl.BlockSpec(memory_space=pltpu.SMEM)
-    dma = pltpu.SemaphoreType.DMA
-    grad_in, grad_w, grad_rel_t = pl.pallas_call(
-        functools.partial(kernel, n_q, n_d, scale_w, scale_r, rel_count, rel_rows),
-        out_shape=(
-            jax.ShapeDtypeStruct((rows, wide), F32),
-            jax.ShapeDtypeStruct((2, feat, feat), F32),
-            jax.ShapeDtypeStruct((2, feat, rel_count), F32),
-        ),
-        in_specs=[vmem] * 7 + [smem] * 2 + [vmem] * 4,
-        out_specs=(vmem, vmem, vmem),
-        scratch_shapes=[
-            pltpu.VMEM((2 * feat, rel_pad), BF16),
-            pltpu.VMEM((n_d, 1, 128), jnp.int32),
-            pltpu.VMEM((rel_pad, edges), BF16),
-            pltpu.VMEM((rows, edges), BF16),
-            pltpu.VMEM((rows, e_in), BF16),
-            pltpu.VMEM((ghosts, e_bd), BF16),
-            pltpu.VMEM((2 * feat, edges), BF16),
-            pltpu.VMEM((wide, edges), BF16),
-            pltpu.VMEM((wide, edges), BF16),
-            pltpu.VMEM((n_d, 1, 128), jnp.int32),
-            pltpu.VMEM((ghosts, wide), BF16),
-            pltpu.VMEM((ghosts, wide), BF16),
-            pltpu.VMEM((ghosts, wide), BF16),
-            pltpu.VMEM((ghosts, wide), BF16),
-            pltpu.VMEM((ghosts, wide), BF16),
-            pltpu.VMEM((ghosts, wide), BF16),
-            pltpu.VMEM((ghosts, wide), BF16),
-            pltpu.VMEM((ghosts, wide), BF16),
-            pltpu.VMEM((2, feat, width), BF16),
-            pltpu.VMEM((2, total, CHUNK, 128), BF16),
-            pltpu.VMEM((2, CHUNK, 128), BF16),
-            pltpu.VMEM((2, feat, width), BF16),
-            dma((5, n_d)),
-            dma((5, n_d)),
-            dma((2, n_chunks)),
-            dma((2, total)),
-            dma((2, total)),
-            dma((2, n_chunks)),
-        ],
-        compiler_params=pltpu.CompilerParams(
-            collective_id=0, has_side_effects=True, vmem_limit_bytes=48 * 1024 * 1024
-        ),
-    )(
+    args = (
         h_in,
         cotangent,
         w_one,
@@ -502,6 +490,62 @@
         edges_in,
         edges_bd,
     )
+    spaces = [pltpu.VMEM] * 7 + [pltpu.SMEM] * 2 + [pltpu.VMEM] * 4
+
+    vmem = pl.BlockSpec(memory_space=pltpu.VMEM)
+    dma = pltpu.SemaphoreType.DMA
+    grad_in, grad_w, grad_rel_t = pl.pallas_call(
+        functools.partial(kernel, n_q, n_d, scale_w, scale_r, rel_count, rel_rows),
+        out_shape=(
+            jax.ShapeDtypeStruct((rows, wide), F32),
+            jax.ShapeDtypeStruct((2, feat, feat), F32),
+            jax.ShapeDtypeStruct((2, feat, rel_count), F32),
+        ),
+        in_specs=[pl.BlockSpec(memory_space=pltpu.HBM)] * len(args),
+        out_specs=(vmem, vmem, vmem),
+        scratch_shapes=[
+            *(space(a.shape, a.dtype) for a, space in zip(args, spaces)),
+            pltpu.VMEM((2 * feat, rel_pad), BF16),
+            pltpu.VMEM((n_d, 1, 128), jnp.int32),
+            pltpu.VMEM((rel_pad, edges), BF16),
+            pltpu.VMEM((rows, edges), BF16),
+            pltpu.VMEM((rows, e_in), BF16),
+            pltpu.VMEM((ghosts, e_bd), BF16),
+            pltpu.VMEM((2 * feat, edges), BF16),
+            pltpu.VMEM((wide, edges), BF16),
+            pltpu.VMEM((wide, edges), BF16),
+            pltpu.VMEM((n_d, 1, 128), jnp.int32),
+            pltpu.VMEM((ghosts, wide), BF16),
+            pltpu.VMEM((ghosts, wide), BF16),
+            pltpu.VMEM((ghosts, wide), BF16),
+            pltpu.VMEM((ghosts, wide), BF16),
+            pltpu.VMEM((ghosts, wide), BF16),
+            pltpu.VMEM((ghosts, wide), BF16),
+            pltpu.VMEM((ghosts, wide), BF16),
+            pltpu.VMEM((ghosts, wide), BF16),
+            pltpu.VMEM((2, feat, width), BF16),
+            pltpu.VMEM((2, total, CHUNK, 128), BF16),
+            pltpu.VMEM((2, CHUNK, 128), BF16),
+            pltpu.VMEM((2, feat, width), BF16),
+            dma((5, n_d)),
+            dma((5, n_d)),
+            dma((2, n_chunks)),
+            dma((2, total)),
+            dma((2, total)),
+            dma((2, n_chunks)),
+            dma((len(args),)),
+        ],
+        compiler_params=pltpu.CompilerParams(
+            collective_id=0, has_side_effects=True, vmem_limit_bytes=48 * 1024 * 1024
+        ),
+    )(*args)
+    grad_in, grad_w, grad_rel_t = pl.pallas_call(
+        write_out,
+        out_shape=tuple(jax.ShapeDtypeStruct(x.shape, x.dtype) for x in (grad_in, grad_w, grad_rel_t)),
+        in_specs=[vmem] * 3,
+        out_specs=[pl.BlockSpec(memory_space=pltpu.HBM)] * 3,
+        scratch_shapes=[dma((3,))],
+    )(grad_in, grad_w, grad_rel_t)
     return grad_in, grad_w, jnp.swapaxes(grad_rel_t, 1, 2)
 
 

time: 54.9 us -> 55.6 us (1.013)
  Pallas kernels: 43 us -> 43.7 us
    pallas_call x0 -> x1, Pallas kernels: none -> 1.89 us  [body(): pl.pallas_call(write_out, out_shape=tuple((jax.ShapeDtypeStruct(x.shape,...]
    pallas_call x1, Pallas kernels: 43 us -> 41.9 us  [body(): pl.pallas_call(functools.partial(kernel, n_q, n_d, scale_w, scale_r, rel_...]
    unnamed x29 -> x32, local copies, waits for them, and re-layouts: 10.6 us -> 10.5 us
where the time goes in v2:
time: 55.6 us; the launch traced here: 55 us
  Pallas kernels  43.7 us (79%)
  local copies, waits for them, and re-layouts  10.5 us (19%)
  between operations  0.69 us (1%)
    pallas_call x1, Pallas kernels, body(): pl.pallas_call(functools.partial(kernel, n_q, n_d, scale_w, scale_r, rel_...  41.9 us
    unnamed x32, local copies, waits for them, and re-layouts  10.5 us
    pallas_call x1, Pallas kernels, body(): pl.pallas_call(write_out, out_shape=tuple((jax.ShapeDtypeStruct(x.shape,...  1.89 us

profile of v2, /device:TPU:0, one launch (start us, length us, event | category | flops | bytes accessed | tf_op | source)
XLA Modules:
  0.0 55.0 jit_solution(10552582098947294787)
XLA Ops:
  0.6 0.0 copy-start.13
  0.6 0.0 copy-start.14
  0.7 0.0 copy-start.15
  0.7 0.6 %copy-done.13 = s32[2]{0:T(128)S(1)} copy-done((s32[2]{0:T(128)S(1)}, s32[2]{0:T(128)}, u32[]{:S(2)}) %copy-start.13) | copy-done | bytes 32
  1.3 0.0 copy-done.14
  1.3 0.0 copy-done.15
  1.3 0.0 copy-start.2
  1.3 0.9 %copy-done.2 = bf16[535,64]{0,1:T(8,128)(2,1)S(1)} copy-done((bf16[535,64]{0,1:T(8,128)(2,1)S(1)}, bf16[535,64]{0,1:T(8,128)(2,1)}, u32[]{:S(2)}) %copy-start.2) | copy-done | bytes 68504
  2.2 0.0 copy-start.3
  2.2 0.9 %copy-done.3 = bf16[535,64]{0,1:T(8,128)(2,1)S(1)} copy-done((bf16[535,64]{0,1:T(8,128)(2,1)S(1)}, bf16[535,64]{0,1:T(8,128)(2,1)}, u32[]{:S(2)}) %copy-start.3) | copy-done | bytes 68504
  3.1 0.0 copy-start.4
  3.1 0.9 %copy-done.4 = bf16[535,64]{0,1:T(8,128)(2,1)S(1)} copy-done((bf16[535,64]{0,1:T(8,128)(2,1)S(1)}, bf16[535,64]{0,1:T(8,128)(2,1)}, u32[]{:S(2)}) %copy-start.4) | copy-done | bytes 68504
  4.0 0.0 copy-start.5
  4.0 0.8 %copy-done.5 = bf16[256,128]{1,0:T(8,128)(2,1)S(1)} copy-done((bf16[256,128]{1,0:T(8,128)(2,1)S(1)}, bf16[256,128]{1,0:T(8,128)(2,1)}, u32[]{:S(2)}) %copy-start.5) | copy-done | bytes 65560
  4.8 0.0 copy-start.6
  4.8 0.8 %copy-done.6 = bf16[256,128]{1,0:T(8,128)(2,1)S(1)} copy-done((bf16[256,128]{1,0:T(8,128)(2,1)S(1)}, bf16[256,128]{1,0:T(8,128)(2,1)}, u32[]{:S(2)}) %copy-start.6) | copy-done | bytes 65560
  5.7 0.0 copy-start.8
  5.7 0.7 %copy-done.8 = bf16[64,64]{1,0:T(8,128)(2,1)S(1)} copy-done((bf16[64,64]{1,0:T(8,128)(2,1)S(1)}, bf16[64,64]{1,0:T(8,128)(2,1)}, u32[]{:S(2)}) %copy-start.8) | copy-done | bytes 8216
  6.4 0.0 copy-start.9
  6.4 0.7 %copy-done.9 = bf16[64,64]{1,0:T(8,128)(2,1)S(1)} copy-done((bf16[64,64]{1,0:T(8,128)(2,1)S(1)}, bf16[64,64]{1,0:T(8,128)(2,1)}, u32[]{:S(2)}) %copy-start.9) | copy-done | bytes 8216
  7.1 0.0 copy-start.10
  7.1 0.7 %copy-done.10 = s32[3,1024]{1,0:T(4,128)S(1)} copy-done((s32[3,1024]{1,0:T(4,128)S(1)}, s32[3,1024]{1,0:T(4,128)}, u32[]{:S(2)}) %copy-start.10) | copy-done | bytes 12312
  7.8 0.0 copy-start.11
  7.8 0.7 %copy-done.11 = s32[3,1024]{1,0:T(4,128)S(1)} copy-done((s32[3,1024]{1,0:T(4,128)S(1)}, s32[3,1024]{1,0:T(4,128)}, u32[]{:S(2)}) %copy-start.11) | copy-done | bytes 12312
  8.5 0.0 copy-start.12
  8.5 0.7 %copy-done.12 = s32[16,16]{1,0:T(8,128)S(1)} copy-done((s32[16,16]{1,0:T(8,128)S(1)}, s32[16,16]{1,0:T(8,128)}, u32[]{:S(2)}) %copy-start.12) | copy-done | bytes 1048
  9.2 41.9 %shard_map.148 = (f32[256,128]{1,0:T(8,128)S(1)}, f32[2,64,64]{2,1,0:T(8,128)S(1)}, f32[2,64,535]{2,1,0:T(8,128)S(1)}) custom-call(bf16[256,128]{1,0:T(8,128)(2,1)S(1)} %copy-done.5, bf16[256,128]{1,0:T(8,128)(2,1)S(1)} %copy-done.6, bf16[64,64]{1,0:T(8,128)(2,1)S(1)} %copy-done.8, bf16[64,64]{1,0:T(8,128)(2,1)S(1)} %copy-done.9, ...), custom_call_target="tpu_custom_call" | custom-call | tf_op jit(solution)/shard_map/pallas_call | solution.py:497
  51.1 0.0 copy-start
  51.1 0.7 %copy-done = f32[2,64,535]{2,1,0:T(8,128)} copy-done((f32[2,64,535]{2,1,0:T(8,128)}, f32[2,64,535]{2,1,0:T(8,128)S(1)}, u32[]{:S(2)}) %copy-start) | copy-done | bytes 273944
  51.8 0.0 copy-start.1
  51.8 0.6 %copy-done.1 = f32[256,128]{1,0:T(8,128)} copy-done((f32[256,128]{1,0:T(8,128)}, f32[256,128]{1,0:T(8,128)S(1)}, u32[]{:S(2)}) %copy-start.1) | copy-done | bytes 131096
  52.5 0.0 copy-start.7
  52.5 0.6 %copy-done.7 = f32[2,64,64]{2,1,0:T(8,128)} copy-done((f32[2,64,64]{2,1,0:T(8,128)}, f32[2,64,64]{2,1,0:T(8,128)S(1)}, u32[]{:S(2)}) %copy-start.7) | copy-done | bytes 32792
  53.1 1.9 %shard_map.149 = (f32[256,128]{1,0:T(8,128)}, f32[2,64,64]{2,1,0:T(8,128)}, f32[2,64,535]{2,1,0:T(8,128)}) custom-call(f32[256,128]{1,0:T(8,128)} %copy-done.1, f32[2,64,64]{2,1,0:T(8,128)} %copy-done.7, f32[2,64,535]{2,1,0:T(8,128)} %copy-done), custom_call_target="tpu_custom_call" | custom-call | tf_op jit(solution)/shard_map/pallas_call | solution.py:542
Async XLA Ops:
  0.6 0.7 %copy-start.13 = (s32[2]{0:T(128)S(1)}, s32[2]{0:T(128)}, u32[]{:S(2)}) copy-start(s32[2]{0:T(128)} %refs_7_.1) | copy-start | bytes 28
  0.6 0.7 %copy-start.14 = (s32[2]{0:T(128)S(1)}, s32[2]{0:T(128)}, u32[]{:S(2)}) copy-start(s32[2]{0:T(128)} %refs_8_.1) | copy-start | bytes 28
  0.7 0.7 %copy-start.15 = (s32[64]{0:T(128)S(1)}, s32[64]{0:T(128)}, u32[]{:S(2)}) copy-start(s32[64]{0:T(128)} %param.22) | copy-start | bytes 772
  1.3 0.9 %copy-start.2 = (bf16[535,64]{0,1:T(8,128)(2,1)S(1)}, bf16[535,64]{0,1:T(8,128)(2,1)}, u32[]{:S(2)}) copy-start(bf16[535,64]{0,1:T(8,128)(2,1)} %param.17) | copy-start | bytes 205444
  2.2 0.9 %copy-start.3 = (bf16[535,64]{0,1:T(8,128)(2,1)S(1)}, bf16[535,64]{0,1:T(8,128)(2,1)}, u32[]{:S(2)}) copy-start(bf16[535,64]{0,1:T(8,128)(2,1)} %param.18) | copy-start | bytes 205444
  3.1 0.9 %copy-start.4 = (bf16[535,64]{0,1:T(8,128)(2,1)S(1)}, bf16[535,64]{0,1:T(8,128)(2,1)}, u32[]{:S(2)}) copy-start(bf16[535,64]{0,1:T(8,128)(2,1)} %param.19) | copy-start | bytes 205444
  4.0 0.8 %copy-start.5 = (bf16[256,128]{1,0:T(8,128)(2,1)S(1)}, bf16[256,128]{1,0:T(8,128)(2,1)}, u32[]{:S(2)}) copy-start(bf16[256,128]{1,0:T(8,128)(2,1)} %refs_0_.1) | copy-start | bytes 196612
  4.8 0.8 %copy-start.6 = (bf16[256,128]{1,0:T(8,128)(2,1)S(1)}, bf16[256,128]{1,0:T(8,128)(2,1)}, u32[]{:S(2)}) copy-start(bf16[256,128]{1,0:T(8,128)(2,1)} %refs_1_.1) | copy-start | bytes 196612
  5.7 0.7 %copy-start.8 = (bf16[64,64]{1,0:T(8,128)(2,1)S(1)}, bf16[64,64]{1,0:T(8,128)(2,1)}, u32[]{:S(2)}) copy-start(bf16[64,64]{1,0:T(8,128)(2,1)} %refs_2_.1) | copy-start | bytes 24580
  6.4 0.7 %copy-start.9 = (bf16[64,64]{1,0:T(8,128)(2,1)S(1)}, bf16[64,64]{1,0:T(8,128)(2,1)}, u32[]{:S(2)}) copy-start(bf16[64,64]{1,0:T(8,128)(2,1)} %refs_3_.1) | copy-start | bytes 24580
  7.1 0.7 %copy-start.10 = (s32[3,1024]{1,0:T(4,128)S(1)}, s32[3,1024]{1,0:T(4,128)}, u32[]{:S(2)}) copy-start(s32[3,1024]{1,0:T(4,128)} %refs_11_.1) | copy-start | bytes 36868
  7.8 0.7 %copy-start.11 = (s32[3,1024]{1,0:T(4,128)S(1)}, s32[3,1024]{1,0:T(4,128)}, u32[]{:S(2)}) copy-start(s32[3,1024]{1,0:T(4,128)} %refs_12_.1) | copy-start | bytes 36868
  8.5 0.7 %copy-start.12 = (s32[16,16]{1,0:T(8,128)S(1)}, s32[16,16]{1,0:T(8,128)}, u32[]{:S(2)}) copy-start(s32[16,16]{1,0:T(8,128)} %refs_10_.1) | copy-start | bytes 3076
  51.1 0.7 %copy-start = (f32[2,64,535]{2,1,0:T(8,128)}, f32[2,64,535]{2,1,0:T(8,128)S(1)}, u32[]{:S(2)}) copy-start(f32[2,64,535]{2,1,0:T(8,128)S(1)} %get-tuple-element.11.refs_2_) | copy-start | bytes 821764
  51.8 0.6 %copy-start.1 = (f32[256,128]{1,0:T(8,128)}, f32[256,128]{1,0:T(8,128)S(1)}, u32[]{:S(2)}) copy-start(f32[256,128]{1,0:T(8,128)S(1)} %get-tuple-element.9.refs_0_) | copy-start | bytes 393220
  52.5 0.6 %copy-start.7 = (f32[2,64,64]{2,1,0:T(8,128)}, f32[2,64,64]{2,1,0:T(8,128)S(1)}, u32[]{:S(2)}) copy-start(f32[2,64,64]{2,1,0:T(8,128)S(1)} %get-tuple-element.10.refs_1_) | copy-start | bytes 98308
